TPU v7x, 32 devices: a whole 2x2x4 slice. The times are simulated.
32 devices in a mesh: gx: 8 (over z, y), pb: 4 (over x, core).
Axes of the slice: x: 2, y: 2, z: 4, core: 2. Of those that a mesh axis runs over, the one named last changes fastest.
Arguments:
- density: float32 [16, 128, 128], P('gx', 'pb'), may hold values from 0.5 to 2
- velocity: float32 [3, 16, 128, 128], P(None, 'gx', 'pb'), may hold values from -3 to 3
- magnetic: float32 [3, 16, 128, 128], P(None, 'gx', 'pb'), may hold values from -4 to 4
- pressure: float32 [16, 128, 128], P('gx', 'pb'), may hold values from 0.2 to 2
- line_owner: int32 [8, 4, 64, 1], P('gx', 'pb'), may hold values from 0 to 7; in each aligned block of 64 rows (0 to 63, 64 to 127, ..., all dimensions but the last counted through in order) at most 16 rows name the same one
- line_row: int32 [8, 4, 64], P('gx', 'pb'), may hold values from 0 to 7
- pedersen: float32 [256, 128], P(('gx', 'pb')), may hold values from 0.5 to 8
- hall: float32 [256, 128], P(('gx', 'pb')), may hold values from 0.3 to 5
- mirror_shift: int32 [256], P(('gx', 'pb')), may hold values from 0 to 127, as said below
Outputs:
- conserved: float32 [8, 16, 128, 128], P(None, 'gx', 'pb')
- potential: float32 [256, 128], P(('gx', 'pb'))
Inputs may be any that keep to these rules, and one draw needn't show every extreme that they name: `line_owner`: among the rows of one device no owner index is named more than 16 times. `mirror_shift`: entry r + 128 equals (128 - entry r) mod 128 for every row r below 128.
All inputs are finite; a program needn't handle non-finite values.
Results may differ from a plain program's by a relative error of at most 0.0003.
Values sent between devices are 32-bit elements; how exact they have to be, the bound alone decides.
A program may use at most 64 MiB of HBM per device.

v0:
```python
import jax
import jax.numpy as jnp
from jax import lax
from jax.sharding import PartitionSpec as P

SWEEPS = 8


GAMMA = 5.0 / 3.0
COURANT = 0.08


def with_halo(cells, sides, width, closed):
    for axis, dim in sides:
        count = lax.axis_size(axis)
        ends = count if closed else count - 1
        head = lax.slice_in_dim(cells, 0, width, axis=dim)
        tail = lax.slice_in_dim(cells, cells.shape[dim] - width, cells.shape[dim], axis=dim)
        cells = jnp.concatenate(
            [
                lax.ppermute(tail, axis, [(i, (i + 1) % count) for i in range(ends)]),
                cells,
                lax.ppermute(head, axis, [((i + 1) % count, i) for i in range(ends)]),
            ],
            axis=dim,
        )
    return cells


def swapped(block, axis, stride):
    count = lax.axis_size(axis)
    route = []
    for low in range(count):
        high = low | 1 << stride
        if high != low and high < count:
            route += [(low, high), (high, low)]
    return lax.ppermute(block, axis, route)


def spatial_slice(values, axis, start, stop):
    return lax.slice_in_dim(values, start, stop, axis=values.ndim - 3 + axis)


def conserved_of(density, velocity, magnetic, pressure):
    field_sq = jnp.sum(magnetic * magnetic, axis=0)
    energy = (
        pressure / (GAMMA - 1.0)
        + 0.5 * density * jnp.sum(velocity * velocity, axis=0)
        + 0.5 * field_sq
    )
    return jnp.concatenate([density[None], density * velocity, magnetic, energy[None]], axis=0)


def direction_flux(density, velocity, magnetic, pressure, d):
    normal_v = velocity[d]
    normal_b = magnetic[d]
    field_sq = jnp.sum(magnetic * magnetic, axis=0)
    total_p = pressure + 0.5 * field_sq
    energy = (
        pressure / (GAMMA - 1.0)
        + 0.5 * density * jnp.sum(velocity * velocity, axis=0)
        + 0.5 * field_sq
    )
    normal_unit = (jnp.arange(3) == d).astype(jnp.float32)[:, None, None, None]
    momentum = density * velocity * normal_v - magnetic * normal_b + normal_unit * total_p
    induced = magnetic * normal_v - normal_b * velocity
    v_dot_b = jnp.sum(velocity * magnetic, axis=0)
    fluxes = jnp.concatenate(
        [
            (density * normal_v)[None],
            momentum,
            induced,
            ((energy + total_p) * normal_v - normal_b * v_dot_b)[None],
        ],
        axis=0,
    )
    sound_sq = GAMMA * pressure / density
    alfven = field_sq / density
    spread = (sound_sq + alfven) ** 2 - 4.0 * sound_sq * normal_b * normal_b / density
    fast_speed = jnp.sqrt(0.5 * (sound_sq + alfven + jnp.sqrt(jnp.maximum(spread, 0.0))))
    return (fluxes, jnp.abs(normal_v) + fast_speed)


def advance(density, velocity, magnetic, pressure):
    conserved_state = conserved_of(density, velocity, magnetic, pressure)
    change = jnp.zeros_like(conserved_state[:, 1:-1, 1:-1, 1:-1])
    for d in range(3):
        fluxes, speeds = direction_flux(density, velocity, magnetic, pressure, d)
        n = density.shape[d]
        lower_flux = spatial_slice(fluxes, d, 0, n - 1)
        upper_flux = spatial_slice(fluxes, d, 1, n)
        lower_state = spatial_slice(conserved_state, d, 0, n - 1)
        upper_state = spatial_slice(conserved_state, d, 1, n)
        largest = jnp.maximum(spatial_slice(speeds, d, 0, n - 1), spatial_slice(speeds, d, 1, n))
        interface = 0.5 * (lower_flux + upper_flux) - 0.5 * largest * (upper_state - lower_state)
        divergence = spatial_slice(interface, d, 1, n - 1) - spatial_slice(interface, d, 0, n - 2)
        for e in range(3):
            if e != d:
                divergence = spatial_slice(divergence, e, 1, density.shape[e] - 1)
        change = change + divergence
    interior = conserved_state[:, 1:-1, 1:-1, 1:-1]
    return interior - COURANT * change


def derivative(values, axis):
    n = values.shape[axis]
    result = (
        lax.slice_in_dim(values, 2, n, axis=axis) - lax.slice_in_dim(values, 0, n - 2, axis=axis)
    ) * 0.5
    for e in range(3):
        if e != axis:
            result = lax.slice_in_dim(result, 1, result.shape[e] - 1, axis=e)
    return result


def aligned_current(field_pad):
    field_x, field_y, field_z = (field_pad[0], field_pad[1], field_pad[2])
    current_x = derivative(field_z, 1) - derivative(field_y, 2)
    current_y = derivative(field_x, 2) - derivative(field_z, 0)
    current_z = derivative(field_y, 0) - derivative(field_x, 1)
    interior = field_pad[:, 1:-1, 1:-1, 1:-1]
    field_size = jnp.sqrt(jnp.sum(interior * interior, axis=0))
    along = current_x * interior[0] + current_y * interior[1] + current_z * interior[2]
    return along / jnp.maximum(field_size, 1.0)


def weights(pedersen_pad, hall_pad):
    pedersen = pedersen_pad[..., 1:-1, :]
    hall = hall_pad[..., 1:-1, :]
    up_ped = pedersen_pad[..., :-2, :]
    down_ped = pedersen_pad[..., 2:, :]
    up_hall = hall_pad[..., :-2, :]
    down_hall = hall_pad[..., 2:, :]
    up_weight = 0.5 * (pedersen + up_ped)
    down_weight = 0.5 * (pedersen + down_ped)
    east_weight = 0.5 * (pedersen + jnp.roll(pedersen, -1, axis=-1))
    west_weight = 0.5 * (pedersen + jnp.roll(pedersen, 1, axis=-1))
    up_east = 0.125 * (hall + jnp.roll(up_hall, -1, axis=-1))
    up_west = 0.125 * (hall + jnp.roll(up_hall, 1, axis=-1))
    down_east = 0.125 * (hall + jnp.roll(down_hall, -1, axis=-1))
    down_west = 0.125 * (hall + jnp.roll(down_hall, 1, axis=-1))
    center = (
        up_weight
        + down_weight
        + east_weight
        + west_weight
        + up_east
        + up_west
        + down_east
        + down_west
    )
    return (
        up_weight,
        down_weight,
        east_weight,
        west_weight,
        up_east,
        -up_west,
        -down_east,
        down_west,
        center,
    )


def sweep(potential_pad, stencil, sources):
    (
        up_weight,
        down_weight,
        east_weight,
        west_weight,
        up_east,
        up_west,
        down_east,
        down_west,
        center,
    ) = stencil
    middle = potential_pad[..., 1:-1, :]
    upper = potential_pad[..., :-2, :]
    lower = potential_pad[..., 2:, :]
    summed = up_weight * upper + down_weight * lower
    summed = (
        summed
        + east_weight * jnp.roll(middle, -1, axis=-1)
        + west_weight * jnp.roll(middle, 1, axis=-1)
    )
    summed = summed + up_east * jnp.roll(upper, -1, axis=-1) + up_west * jnp.roll(upper, 1, axis=-1)
    summed = (
        summed + down_east * jnp.roll(lower, -1, axis=-1) + down_west * jnp.roll(lower, 1, axis=-1)
    )
    return (summed + sources) / center


def couple(local_phi, partner_phi, local_ped, partner_ped, shifts):
    n = local_phi.shape[-1]
    columns = (jnp.arange(n, dtype=jnp.int32)[None, :] + shifts[:, None]) % n
    mirrored = jnp.take_along_axis(partner_phi, columns, axis=-1)
    mirrored_ped = jnp.take_along_axis(partner_ped, columns, axis=-1)
    return (local_ped * local_phi + mirrored_ped * mirrored) / (local_ped + mirrored_ped)


def edge_copy(values, axis, width, position, count):
    n = values.shape[axis]
    first = lax.slice_in_dim(values, width, width + 1, axis=axis)
    last = lax.slice_in_dim(values, n - width - 1, n - width, axis=axis)
    lower = lax.slice_in_dim(values, 0, width, axis=axis)
    upper = lax.slice_in_dim(values, n - width, n, axis=axis)
    middle = lax.slice_in_dim(values, width, n - width, axis=axis)
    lower = jnp.where(position == 0, first, lower)
    upper = jnp.where(position == count - 1, last, upper)
    return jnp.concatenate([lower, middle, upper], axis=axis)


def pad_depth(values):
    widths = [(0, 0)] * (values.ndim - 1) + [(1, 1)]
    return jnp.pad(values, widths, mode="edge")


def advance_block(widened):
    widened = pad_depth(widened)
    return advance(widened[0], widened[1:4], widened[4:7], widened[7])


def body(density, velocity, magnetic, pressure, line_owner, line_row, pedersen, hall, mirror_shift):
    x_index = lax.axis_index("gx")
    x_count = lax.axis_size("gx")
    y_index = lax.axis_index("pb")
    y_count = lax.axis_size("pb")
    primitive = jnp.concatenate([density[None], velocity, magnetic, pressure[None]], axis=0)
    widened = with_halo(primitive, (("gx", 1), ("pb", 2)), 1, False)
    widened = edge_copy(widened, 1, 1, x_index, x_count)
    widened = edge_copy(widened, 2, 1, y_index, y_count)
    updated = advance_block(widened)
    field_pad = with_halo(updated[4:7], (("gx", 1), ("pb", 2)), 1, False)
    field_pad = edge_copy(field_pad, 1, 1, x_index, x_count)
    field_pad = edge_copy(field_pad, 2, 1, y_index, y_count)
    current = aligned_current(pad_depth(field_pad))
    rows_dev = current.shape[0] * current.shape[1]
    depth = current.shape[2]
    current_rows = current.reshape(rows_dev, depth)
    owners = line_owner.reshape(rows_dev)
    targets = line_row.reshape(rows_dev)
    capacity = max(2, 2 * rows_dev // x_count)
    owner_hot = (owners[:, None] == jnp.arange(x_count, dtype=jnp.int32)[None, :]).astype(jnp.int32)
    earlier = jnp.cumsum(owner_hot, axis=0) - owner_hot
    place_in = jnp.sum(earlier * owner_hot, axis=1)
    slot_number = owners * capacity + place_in
    slot_hot = (
        slot_number[:, None] == jnp.arange(x_count * capacity, dtype=jnp.int32)[None, :]
    ).astype(jnp.float32)
    outgoing = jnp.dot(
        slot_hot.T,
        current_rows,
        precision=lax.Precision.HIGHEST,
        preferred_element_type=jnp.float32,
    ).reshape(x_count, capacity, depth)
    labels = jnp.dot(
        slot_hot.T,
        (targets + 1).astype(jnp.float32),
        precision=lax.Precision.HIGHEST,
        preferred_element_type=jnp.float32,
    ).reshape(x_count, capacity)
    arrived, arrived_labels = (
        lax.all_to_all(outgoing, "gx", split_axis=0, concat_axis=0, tiled=True),
        lax.all_to_all(labels, "gx", split_axis=0, concat_axis=0, tiled=True),
    )
    rows_ion = pedersen.shape[0]
    deposit_hot = (
        (arrived_labels.reshape(-1) - 1.0)[None, :]
        == jnp.arange(rows_ion, dtype=jnp.float32)[:, None]
    ).astype(jnp.float32)
    sources = jnp.dot(
        deposit_hot,
        arrived.reshape(-1, depth),
        precision=lax.Precision.HIGHEST,
        preferred_element_type=jnp.float32,
    )
    flat_index = x_index * y_count + y_index
    half_count = x_count * y_count // 2
    quarter_count = half_count // 2
    band_place = flat_index % half_count

    def latitude_fix(padded):
        lower = padded[..., :1, :]
        upper = padded[..., -1:, :]
        lower = jnp.where(band_place == quarter_count, jnp.zeros_like(lower), lower)
        upper = jnp.where(band_place == quarter_count - 1, jnp.zeros_like(upper), upper)
        return jnp.concatenate([lower, padded[..., 1:-1, :], upper], axis=-2)

    top_bit = x_count.bit_length() - 2
    longitude = pedersen.shape[1]
    cond_pad = latitude_fix(with_halo(jnp.stack([pedersen, hall]), ((("gx", "pb"), 1),), 1, True))
    stencil = weights(cond_pad[0], cond_pad[1])
    partner_ped = swapped(pedersen, "gx", top_bit)
    potential = jnp.zeros((rows_ion, longitude), jnp.float32)
    for repeat in range(SWEEPS):
        padded = latitude_fix(with_halo(potential, ((("gx", "pb"), 0),), 1, True))
        potential = sweep(padded, stencil, sources)
        partner_phi = swapped(potential, "gx", top_bit)
        potential = couple(potential, partner_phi, pedersen, partner_ped, mirror_shift)
    return (updated, potential)


def solution(mesh):
    in_specs = (
        P("gx", "pb", None),
        P(None, "gx", "pb", None),
        P(None, "gx", "pb", None),
        P("gx", "pb", None),
        P("gx", "pb", None, None),
        P("gx", "pb", None),
        P(("gx", "pb"), None),
        P(("gx", "pb"), None),
        P(("gx", "pb")),
    )
    out_specs = (P(None, "gx", "pb", None), P(("gx", "pb"), None))
    return jax.shard_map(body, mesh=mesh, in_specs=in_specs, out_specs=out_specs, check_vma=False)
```

profile of v0, /device:TPU:0, one launch (start us, length us, event | category | flops | bytes accessed | tf_op | source)
XLA Modules:
  0.0 194.3 jit_solution(15178667991943477502)
XLA Ops:
  1.2 6.0 %collective-permute-start.7 = (f32[1,128]{1,0:T(1,128)S(1)}, f32[1,128]{1,0:T(1,128)S(1)}, u32[]{:S(2)}, u32[]{:S(2)}) collective-permute-start(f32[1,128]{1,0:T(1,128)S(1)} %broadcast.193), channel_id=1, source_target_pairs={{1,0},{2,1},{3,2},{4,3},{5,4},{6,5},{7,6},{8,7},{9,8},{10,9},{11,1... | collective-permute-start | bytes 1544 | tf_op jit(solution)/shard_map/ppermute | solution.py:23
  7.2 1.0 pad_maximum_fusion.9
  8.2 1.3 collective-permute-start.1
  9.5 4.6 %collective-permute-start = (f32[8,1,32,128]{3,2,1,0:T(8,128)S(1)}, f32[8,1,32,128]{3,2,1,0:T(8,128)S(1)}, u32[]{:S(2)}, u32[]{:S(2)}) collective-permute-start(f32[8,1,32,128]{3,2,1,0:T(8,128)S(1)} %get-tuple-element.70), channel_id=1, source_target_pairs={{0,4},{4,8},{8,12},{12,16},{16,20},{20,24},{24,28},{1,5},{5,9},{9,... | collective-permute-start | bytes 393224 | tf_op jit(solution)/shard_map/ppermute | solution.py:21
  14.9 0.8 select_reduce_fusion
  16.4 1.7 convolution_bitcast_fusion
  18.1 3.4 %all-to-all-start = ((f32[8,1,16]{2,1,0:T(1,128)}), f32[8,1,16]{2,1,0:T(1,128)S(1)}, u32[]{:S(2)}, u32[]{:S(2)}) async-start(f32[8,1,16]{2,1,0:T(1,128)} %convolution_bitcast_fusion), calls=%async_computation | async-start | bytes 8192 | tf_op jit(solution)/shard_map/all_to_all | solution.py:264
  21.5 2.9 %collective-permute-start.12 = (f32[8,128]{1,0:T(8,128)}, f32[8,128]{1,0:T(8,128)S(1)}, u32[]{:S(2)}, u32[]{:S(2)}) collective-permute-start(f32[8,128]{1,0:T(8,128)} %param.17), channel_id=1, source_target_pairs={{0,16},{16,0},{4,20},{20,4},{8,24},{24,8},{12,28},{28,12},{1,17},{... | collective-permute-start | bytes 12296 | tf_op jit(solution)/shard_map/ppermute | solution.py:37
  25.6 2.3 %all-to-all-done = f32[8,1,16]{2,1,0:T(1,128)S(1)} async-done(((f32[8,1,16]{2,1,0:T(1,128)}), f32[8,1,16]{2,1,0:T(1,128)S(1)}, u32[]{:S(2)}, u32[]{:S(2)}) %all-to-all-start) | async-done | bytes 544 | tf_op jit(solution)/shard_map/all_to_all | solution.py:264
  28.0 3.9 %collective-permute-done.4 = f32[2,1,128]{2,1,0:T(1,128)S(1)} collective-permute-done((f32[2,1,128]{2,1,0:T(1,128)S(1)}, f32[2,1,128]{2,1,0:T(1,128)S(1)}, u32[]{:S(2)}, u32[]{:S(2)}) %collective-permute-start.4) | collective-permute-done | bytes 1056 | tf_op jit(solution)/shard_map/ppermute | solution.py:21
  32.0 1.3 collective-permute-start.3
  33.3 3.0 %collective-permute-start.2 = (f32[8,4,1,128]{3,2,1,0:T(1,128)S(1)}, f32[8,4,1,128]{3,2,1,0:T(1,128)S(1)}, u32[]{:S(2)}, u32[]{:S(2)}) collective-permute-start(f32[8,4,1,128]{3,2,1,0:T(1,128)S(1)} %get-tuple-element.59), channel_id=1, source_target_pairs={{0,1},{1,2},{2,3},{4,5},{5,6},{6,7},{8,9},{9,10},{10,11},{12,13},{... | collective-permute-start | bytes 49160 | tf_op jit(solution)/shard_map/ppermute | solution.py:21
  36.3 0.8 collective-permute-done.2
  43.0 1.3 collective-permute-start.9
  44.3 4.5 %collective-permute-start.8 = (f32[3,1,32,128]{3,2,1,0:T(8,128)S(1)}, f32[3,1,32,128]{3,2,1,0:T(8,128)S(1)}, u32[]{:S(2)}, u32[]{:S(2)}) collective-permute-start(f32[3,1,32,128]{3,2,1,0:T(8,128)S(1)} %get-tuple-element.68), channel_id=1, source_target_pairs={{0,4},{4,8},{8,12},{12,16},{16,20},{20,24},{24,28},{1,5},{5,9},{9,... | collective-permute-start | bytes 147464 | tf_op jit(solution)/shard_map/ppermute | solution.py:21
  49.0 1.6 collective-permute-done.8
  50.6 1.3 collective-permute-start.11
  51.9 3.0 %collective-permute-start.10 = (f32[3,4,1,128]{3,2,1,0:T(1,128)S(1)}, f32[3,4,1,128]{3,2,1,0:T(1,128)S(1)}, u32[]{:S(2)}, u32[]{:S(2)}) collective-permute-start(f32[3,4,1,128]{3,2,1,0:T(1,128)S(1)} %get-tuple-element.78), channel_id=1, source_target_pairs={{0,1},{1,2},{2,3},{4,5},{5,6},{6,7},{8,9},{9,10},{10,11},{12,13},{... | collective-permute-start | bytes 18440 | tf_op jit(solution)/shard_map/ppermute | solution.py:21
  56.8 0.8 fusion.38
  57.7 3.6 %all-to-all-start.1 = ((f32[8,16,128]{2,1,0:T(8,128)}), f32[8,16,128]{2,1,0:T(8,128)S(1)}, u32[]{:S(2)}, u32[]{:S(2)}) async-start(f32[8,16,128]{2,1,0:T(8,128)} %fusion.38), calls=%async_computation.1 | async-start | bytes 131072 | tf_op jit(solution)/shard_map/all_to_all | solution.py:263
  61.4 6.8 %all-to-all-done.1 = f32[8,16,128]{2,1,0:T(8,128)S(1)} async-done(((f32[8,16,128]{2,1,0:T(8,128)}), f32[8,16,128]{2,1,0:T(8,128)S(1)}, u32[]{:S(2)}, u32[]{:S(2)}) %all-to-all-start.1) | async-done | bytes 65568 | tf_op jit(solution)/shard_map/all_to_all | solution.py:263
  69.0 4.5 %gather_fusion = f32[1024]{0:T(1024)S(1)} fusion(f32[8,128]{1,0:T(8,128)S(1)} %collective-permute-done.12, s32[1024]{0:T(1024)S(1)} %fusion.271), kind=kCustom, calls=%fused_computation.clone | custom fusion | bytes 16384 | tf_op jit(solution)/shard_map/jit(take_along_axis)/gather | solution.py:197
  73.5 4.5 %gather_fusion.1 = f32[1024]{0:T(1024)S(1)} fusion(f32[8,128]{1,0:T(8,128)S(1)} %collective-permute-done.13, s32[1024]{0:T(1024)S(1)} %fusion.271), kind=kCustom, calls=%fused_computation.1.clone | custom fusion | bytes 16384 | tf_op jit(solution)/shard_map/jit(take_along_axis)/gather | solution.py:196
  78.2 2.7 %collective-permute-start.15 = (f32[1,128]{1,0:T(1,128)S(1)}, f32[1,128]{1,0:T(1,128)S(1)}, u32[]{:S(2)}, u32[]{:S(2)}) collective-permute-start(f32[1,128]{1,0:T(1,128)S(1)} %get-tuple-element.189), channel_id=1, source_target_pairs={{1,0},{2,1},{3,2},{4,3},{5,4},{6,5},{7,6},{8,7},{9,8},{10,9},{11,1... | collective-permute-start | bytes 1544 | tf_op jit(solution)/shard_map/ppermute | solution.py:23
  80.9 1.3 collective-permute-done.15
  82.2 5.3 %collective-permute-done.14 = f32[1,128]{1,0:T(1,128)S(1)} collective-permute-done((f32[1,128]{1,0:T(1,128)S(1)}, f32[1,128]{1,0:T(1,128)S(1)}, u32[]{:S(2)}, u32[]{:S(2)}) %collective-permute-start.14) | collective-permute-done | bytes 544 | tf_op jit(solution)/shard_map/ppermute | solution.py:21
  87.7 4.5 %collective-permute-done.16 = f32[8,128]{1,0:T(8,128)S(1)} collective-permute-done((f32[8,128]{1,0:T(8,128)S(1)}, f32[8,128]{1,0:T(8,128)S(1)}, u32[]{:S(2)}, u32[]{:S(2)}) %collective-permute-start.16) | collective-permute-done | bytes 4128 | tf_op jit(solution)/shard_map/ppermute | solution.py:37
  92.2 4.5 %gather_fusion.2 = f32[1024]{0:T(1024)S(1)} fusion(f32[8,128]{1,0:T(8,128)S(1)} %collective-permute-done.16, s32[1024]{0:T(1024)S(1)} %fusion.271), kind=kCustom, calls=%fused_computation.2.clone | custom fusion | bytes 16384 | tf_op jit(solution)/shard_map/jit(take_along_axis)/gather | solution.py:196
  98.2 5.3 %collective-permute-done.17 = f32[1,128]{1,0:T(1,128)S(1)} collective-permute-done((f32[1,128]{1,0:T(1,128)S(1)}, f32[1,128]{1,0:T(1,128)S(1)}, u32[]{:S(2)}, u32[]{:S(2)}) %collective-permute-start.17) | collective-permute-done | bytes 544 | tf_op jit(solution)/shard_map/ppermute | solution.py:21
  103.9 4.5 %collective-permute-done.19 = f32[8,128]{1,0:T(8,128)S(1)} collective-permute-done((f32[8,128]{1,0:T(8,128)S(1)}, f32[8,128]{1,0:T(8,128)S(1)}, u32[]{:S(2)}, u32[]{:S(2)}) %collective-permute-start.19) | collective-permute-done | bytes 4128 | tf_op jit(solution)/shard_map/ppermute | solution.py:37
  108.4 4.5 %gather_fusion.3 = f32[1024]{0:T(1024)S(1)} fusion(f32[8,128]{1,0:T(8,128)S(1)} %collective-permute-done.19, s32[1024]{0:T(1024)S(1)} %fusion.271), kind=kCustom, calls=%fused_computation.3.clone | custom fusion | bytes 16384 | tf_op jit(solution)/shard_map/jit(take_along_axis)/gather | solution.py:196
  114.4 5.3 %collective-permute-done.20 = f32[1,128]{1,0:T(1,128)S(1)} collective-permute-done((f32[1,128]{1,0:T(1,128)S(1)}, f32[1,128]{1,0:T(1,128)S(1)}, u32[]{:S(2)}, u32[]{:S(2)}) %collective-permute-start.20) | collective-permute-done | bytes 544 | tf_op jit(solution)/shard_map/ppermute | solution.py:21
  120.0 4.5 %collective-permute-done.22 = f32[8,128]{1,0:T(8,128)S(1)} collective-permute-done((f32[8,128]{1,0:T(8,128)S(1)}, f32[8,128]{1,0:T(8,128)S(1)}, u32[]{:S(2)}, u32[]{:S(2)}) %collective-permute-start.22) | collective-permute-done | bytes 4128 | tf_op jit(solution)/shard_map/ppermute | solution.py:37
  124.5 4.5 %gather_fusion.4 = f32[1024]{0:T(1024)S(1)} fusion(f32[8,128]{1,0:T(8,128)S(1)} %collective-permute-done.22, s32[1024]{0:T(1024)S(1)} %fusion.271), kind=kCustom, calls=%fused_computation.4.clone | custom fusion | bytes 16384 | tf_op jit(solution)/shard_map/jit(take_along_axis)/gather | solution.py:196
  129.7 0.8 collective-permute-done.24
  130.5 5.3 %collective-permute-done.23 = f32[1,128]{1,0:T(1,128)S(1)} collective-permute-done((f32[1,128]{1,0:T(1,128)S(1)}, f32[1,128]{1,0:T(1,128)S(1)}, u32[]{:S(2)}, u32[]{:S(2)}) %collective-permute-start.23) | collective-permute-done | bytes 544 | tf_op jit(solution)/shard_map/ppermute | solution.py:21
  136.2 4.5 %collective-permute-done.25 = f32[8,128]{1,0:T(8,128)S(1)} collective-permute-done((f32[8,128]{1,0:T(8,128)S(1)}, f32[8,128]{1,0:T(8,128)S(1)}, u32[]{:S(2)}, u32[]{:S(2)}) %collective-permute-start.25) | collective-permute-done | bytes 4128 | tf_op jit(solution)/shard_map/ppermute | solution.py:37
  140.7 4.5 %gather_fusion.5 = f32[1024]{0:T(1024)S(1)} fusion(f32[8,128]{1,0:T(8,128)S(1)} %collective-permute-done.25, s32[1024]{0:T(1024)S(1)} %fusion.271), kind=kCustom, calls=%fused_computation.5.clone | custom fusion | bytes 16384 | tf_op jit(solution)/shard_map/jit(take_along_axis)/gather | solution.py:196
  145.9 0.8 collective-permute-done.27
  146.7 5.3 %collective-permute-done.26 = f32[1,128]{1,0:T(1,128)S(1)} collective-permute-done((f32[1,128]{1,0:T(1,128)S(1)}, f32[1,128]{1,0:T(1,128)S(1)}, u32[]{:S(2)}, u32[]{:S(2)}) %collective-permute-start.26) | collective-permute-done | bytes 544 | tf_op jit(solution)/shard_map/ppermute | solution.py:21
  152.3 4.5 %collective-permute-done.28 = f32[8,128]{1,0:T(8,128)S(1)} collective-permute-done((f32[8,128]{1,0:T(8,128)S(1)}, f32[8,128]{1,0:T(8,128)S(1)}, u32[]{:S(2)}, u32[]{:S(2)}) %collective-permute-start.28) | collective-permute-done | bytes 4128 | tf_op jit(solution)/shard_map/ppermute | solution.py:37
  156.8 4.5 %gather_fusion.6 = f32[1024]{0:T(1024)S(1)} fusion(f32[8,128]{1,0:T(8,128)S(1)} %collective-permute-done.28, s32[1024]{0:T(1024)S(1)} %fusion.271), kind=kCustom, calls=%fused_computation.6.clone | custom fusion | bytes 16384 | tf_op jit(solution)/shard_map/jit(take_along_axis)/gather | solution.py:196
  162.8 5.3 %collective-permute-done.29 = f32[1,128]{1,0:T(1,128)S(1)} collective-permute-done((f32[1,128]{1,0:T(1,128)S(1)}, f32[1,128]{1,0:T(1,128)S(1)}, u32[]{:S(2)}, u32[]{:S(2)}) %collective-permute-start.29) | collective-permute-done | bytes 544 | tf_op jit(solution)/shard_map/ppermute | solution.py:21
  168.5 4.5 %collective-permute-done.31 = f32[8,128]{1,0:T(8,128)S(1)} collective-permute-done((f32[8,128]{1,0:T(8,128)S(1)}, f32[8,128]{1,0:T(8,128)S(1)}, u32[]{:S(2)}, u32[]{:S(2)}) %collective-permute-start.31) | collective-permute-done | bytes 4128 | tf_op jit(solution)/shard_map/ppermute | solution.py:37
  173.0 4.5 %gather_fusion.7 = f32[1024]{0:T(1024)S(1)} fusion(f32[8,128]{1,0:T(8,128)S(1)} %collective-permute-done.31, s32[1024]{0:T(1024)S(1)} %fusion.271), kind=kCustom, calls=%fused_computation.7.clone | custom fusion | bytes 16384 | tf_op jit(solution)/shard_map/jit(take_along_axis)/gather | solution.py:196
  179.0 5.3 %collective-permute-done.32 = f32[1,128]{1,0:T(1,128)S(1)} collective-permute-done((f32[1,128]{1,0:T(1,128)S(1)}, f32[1,128]{1,0:T(1,128)S(1)}, u32[]{:S(2)}, u32[]{:S(2)}) %collective-permute-start.32) | collective-permute-done | bytes 544 | tf_op jit(solution)/shard_map/ppermute | solution.py:21
  184.6 4.5 %collective-permute-done.34 = f32[8,128]{1,0:T(8,128)S(1)} collective-permute-done((f32[8,128]{1,0:T(8,128)S(1)}, f32[8,128]{1,0:T(8,128)S(1)}, u32[]{:S(2)}, u32[]{:S(2)}) %collective-permute-start.34) | collective-permute-done | bytes 4128 | tf_op jit(solution)/shard_map/ppermute | solution.py:37
  189.1 4.5 %gather_fusion.8 = f32[1024]{0:T(1024)S(1)} fusion(f32[8,128]{1,0:T(8,128)S(1)} %collective-permute-done.34, s32[1024]{0:T(1024)S(1)} %fusion.271), kind=kCustom, calls=%fused_computation.8.clone | custom fusion | bytes 16384 | tf_op jit(solution)/shard_map/jit(take_along_axis)/gather | solution.py:196
  (182 shorter events, 21.7 us)
Async XLA Ops:
  0.6 31.3 %copy-start.4 = (f32[2,32,128]{2,1,0:T(8,128)S(1)}, f32[2,32,128]{2,1,0:T(8,128)}, u32[]{:S(2)}) copy-start(f32[2,32,128]{2,1,0:T(8,128)} %param.14) | copy-start | bytes 98308
  0.6 31.3 %copy-start.2 = (f32[3,2,32,128]{3,2,1,0:T(8,128)S(1)}, f32[3,2,32,128]{3,2,1,0:T(8,128)}, u32[]{:S(2)}) copy-start(f32[3,2,32,128]{3,2,1,0:T(8,128)} %param.13) | copy-start | bytes 294916
  0.7 31.3 %copy-start.3 = (f32[3,2,32,128]{3,2,1,0:T(8,128)S(1)}, f32[3,2,32,128]{3,2,1,0:T(8,128)}, u32[]{:S(2)}) copy-start(f32[3,2,32,128]{3,2,1,0:T(8,128)} %param.12) | copy-start | bytes 294916
  0.7 31.3 %copy-start.5 = (f32[2,32,128]{2,1,0:T(8,128)S(1)}, f32[2,32,128]{2,1,0:T(8,128)}, u32[]{:S(2)}) copy-start(f32[2,32,128]{2,1,0:T(8,128)} %param.11) | copy-start | bytes 98308
  0.7 23.8 %copy-start.1 = (f32[8,128]{1,0:T(8,128)S(1)}, f32[8,128]{1,0:T(8,128)}, u32[]{:S(2)}) copy-start(f32[8,128]{1,0:T(8,128)} %param.17) | copy-start | bytes 12292
  0.7 23.9 %copy-start.6 = (f32[8,128]{1,0:T(8,128)S(1)}, f32[8,128]{1,0:T(8,128)}, u32[]{:S(2)}) copy-start(f32[8,128]{1,0:T(8,128)} %param.18) | copy-start | bytes 12292
  0.7 24.0 %collective-permute-start.5 = (f32[1,128]{1,0:T(1,128)S(1)}, f32[1,128]{1,0:T(1,128)S(1)}, u32[]{:S(2)}, u32[]{:S(2)}) collective-permute-start(f32[1,128]{1,0:T(1,128)S(1)} %broadcast.193), channel_id=1, source_target_pairs={{0,1},{1,2},{2,3},{3,4},{4,5},{5,6},{6,7},{7,8},{8,9},{9,10},{10,1... | collective-permute-start | bytes 1544 | tf_op jit(solution)/shard_map/ppermute | solution.py:21
  1.2 24.1 %collective-permute-start.7 = (f32[1,128]{1,0:T(1,128)S(1)}, f32[1,128]{1,0:T(1,128)S(1)}, u32[]{:S(2)}, u32[]{:S(2)}) collective-permute-start(f32[1,128]{1,0:T(1,128)S(1)} %broadcast.193), channel_id=1, source_target_pairs={{1,0},{2,1},{3,2},{4,3},{5,4},{6,5},{7,6},{8,7},{9,8},{10,9},{11,1... | collective-permute-start | bytes 1544 | tf_op jit(solution)/shard_map/ppermute | solution.py:23
  8.2 23.7 %collective-permute-start.1 = (f32[8,1,32,128]{3,2,1,0:T(8,128)S(1)}, f32[8,1,32,128]{3,2,1,0:T(8,128)S(1)}, u32[]{:S(2)}, u32[]{:S(2)}) collective-permute-start(f32[8,1,32,128]{3,2,1,0:T(8,128)S(1)} %get-tuple-element.71), channel_id=1, source_target_pairs={{4,0},{8,4},{12,8},{16,12},{20,16},{24,20},{28,24},{5,1},{9,5},{13... | collective-permute-start | bytes 393224 | tf_op jit(solution)/shard_map/ppermute | solution.py:23
  9.5 22.4 %collective-permute-start = (f32[8,1,32,128]{3,2,1,0:T(8,128)S(1)}, f32[8,1,32,128]{3,2,1,0:T(8,128)S(1)}, u32[]{:S(2)}, u32[]{:S(2)}) collective-permute-start(f32[8,1,32,128]{3,2,1,0:T(8,128)S(1)} %get-tuple-element.70), channel_id=1, source_target_pairs={{0,4},{4,8},{8,12},{12,16},{16,20},{20,24},{24,28},{1,5},{5,9},{9,... | collective-permute-start | bytes 393224 | tf_op jit(solution)/shard_map/ppermute | solution.py:21
  18.1 9.8 %all-to-all-start = ((f32[8,1,16]{2,1,0:T(1,128)}), f32[8,1,16]{2,1,0:T(1,128)S(1)}, u32[]{:S(2)}, u32[]{:S(2)}) async-start(f32[8,1,16]{2,1,0:T(1,128)} %convolution_bitcast_fusion), calls=%async_computation | async-start | bytes 8192 | tf_op jit(solution)/shard_map/all_to_all | solution.py:264
  21.5 47.4 %collective-permute-start.12 = (f32[8,128]{1,0:T(8,128)}, f32[8,128]{1,0:T(8,128)S(1)}, u32[]{:S(2)}, u32[]{:S(2)}) collective-permute-start(f32[8,128]{1,0:T(8,128)} %param.17), channel_id=1, source_target_pairs={{0,16},{16,0},{4,20},{20,4},{8,24},{24,8},{12,28},{28,12},{1,17},{... | collective-permute-start | bytes 12296 | tf_op jit(solution)/shard_map/ppermute | solution.py:37
  24.7 3.3 %collective-permute-start.6 = (f32[2,1,128]{2,1,0:T(1,128)S(1)}, f32[2,1,128]{2,1,0:T(1,128)S(1)}, u32[]{:S(2)}, u32[]{:S(2)}) collective-permute-start(f32[2,1,128]{2,1,0:T(1,128)S(1)} %get-tuple-element.90), channel_id=1, source_target_pairs={{1,0},{2,1},{3,2},{4,3},{5,4},{6,5},{7,6},{8,7},{9,8},{10,9},{11,1... | collective-permute-start | bytes 3080 | tf_op jit(solution)/shard_map/ppermute | solution.py:23
  25.3 6.6 %collective-permute-start.4 = (f32[2,1,128]{2,1,0:T(1,128)S(1)}, f32[2,1,128]{2,1,0:T(1,128)S(1)}, u32[]{:S(2)}, u32[]{:S(2)}) collective-permute-start(f32[2,1,128]{2,1,0:T(1,128)S(1)} %get-tuple-element.91), channel_id=1, source_target_pairs={{0,1},{1,2},{2,3},{3,4},{4,5},{5,6},{6,7},{7,8},{8,9},{9,10},{10,1... | collective-permute-start | bytes 3080 | tf_op jit(solution)/shard_map/ppermute | solution.py:21
  32.0 4.4 %collective-permute-start.3 = (f32[8,4,1,128]{3,2,1,0:T(1,128)S(1)}, f32[8,4,1,128]{3,2,1,0:T(1,128)S(1)}, u32[]{:S(2)}, u32[]{:S(2)}) collective-permute-start(f32[8,4,1,128]{3,2,1,0:T(1,128)S(1)} %get-tuple-element.60), channel_id=1, source_target_pairs={{1,0},{2,1},{3,2},{5,4},{6,5},{7,6},{9,8},{10,9},{11,10},{13,12},{... | collective-permute-start | bytes 49160 | tf_op jit(solution)/shard_map/ppermute | solution.py:23
  33.3 3.9 %collective-permute-start.2 = (f32[8,4,1,128]{3,2,1,0:T(1,128)S(1)}, f32[8,4,1,128]{3,2,1,0:T(1,128)S(1)}, u32[]{:S(2)}, u32[]{:S(2)}) collective-permute-start(f32[8,4,1,128]{3,2,1,0:T(1,128)S(1)} %get-tuple-element.59), channel_id=1, source_target_pairs={{0,1},{1,2},{2,3},{4,5},{5,6},{6,7},{8,9},{9,10},{10,11},{12,13},{... | collective-permute-start | bytes 49160 | tf_op jit(solution)/shard_map/ppermute | solution.py:21
  42.9 13.7 %copy-start = (f32[8,2,32,128]{3,2,1,0:T(8,128)}, f32[8,2,32,128]{3,2,1,0:T(8,128)S(1)}, u32[]{:S(2)}) copy-start(f32[8,2,32,128]{3,2,1,0:T(8,128)S(1)} %fusion.11) | copy-start | bytes 786436
  43.0 6.0 %collective-permute-start.9 = (f32[3,1,32,128]{3,2,1,0:T(8,128)S(1)}, f32[3,1,32,128]{3,2,1,0:T(8,128)S(1)}, u32[]{:S(2)}, u32[]{:S(2)}) collective-permute-start(f32[3,1,32,128]{3,2,1,0:T(8,128)S(1)} %get-tuple-element.69), channel_id=1, source_target_pairs={{4,0},{8,4},{12,8},{16,12},{20,16},{24,20},{28,24},{5,1},{9,5},{13... | collective-permute-start | bytes 147464 | tf_op jit(solution)/shard_map/ppermute | solution.py:23
  44.3 6.3 %collective-permute-start.8 = (f32[3,1,32,128]{3,2,1,0:T(8,128)S(1)}, f32[3,1,32,128]{3,2,1,0:T(8,128)S(1)}, u32[]{:S(2)}, u32[]{:S(2)}) collective-permute-start(f32[3,1,32,128]{3,2,1,0:T(8,128)S(1)} %get-tuple-element.68), channel_id=1, source_target_pairs={{0,4},{4,8},{8,12},{12,16},{16,20},{20,24},{24,28},{1,5},{5,9},{9,... | collective-permute-start | bytes 147464 | tf_op jit(solution)/shard_map/ppermute | solution.py:21
  50.6 4.4 %collective-permute-start.11 = (f32[3,4,1,128]{3,2,1,0:T(1,128)S(1)}, f32[3,4,1,128]{3,2,1,0:T(1,128)S(1)}, u32[]{:S(2)}, u32[]{:S(2)}) collective-permute-start(f32[3,4,1,128]{3,2,1,0:T(1,128)S(1)} %get-tuple-element.79), channel_id=1, source_target_pairs={{1,0},{2,1},{3,2},{5,4},{6,5},{7,6},{9,8},{10,9},{11,10},{13,12},{... | collective-permute-start | bytes 18440 | tf_op jit(solution)/shard_map/ppermute | solution.py:23
  51.9 3.8 %collective-permute-start.10 = (f32[3,4,1,128]{3,2,1,0:T(1,128)S(1)}, f32[3,4,1,128]{3,2,1,0:T(1,128)S(1)}, u32[]{:S(2)}, u32[]{:S(2)}) collective-permute-start(f32[3,4,1,128]{3,2,1,0:T(1,128)S(1)} %get-tuple-element.78), channel_id=1, source_target_pairs={{0,1},{1,2},{2,3},{4,5},{5,6},{6,7},{8,9},{9,10},{10,11},{12,13},{... | collective-permute-start | bytes 18440 | tf_op jit(solution)/shard_map/ppermute | solution.py:21
  56.4 12.4 %copy-start.7 = (s32[8]{0:T(128)S(1)}, s32[8]{0:T(128)}, u32[]{:S(2)}) copy-start(s32[8]{0:T(128)} %param.19) | copy-start | bytes 100
  57.7 10.5 %all-to-all-start.1 = ((f32[8,16,128]{2,1,0:T(8,128)}), f32[8,16,128]{2,1,0:T(8,128)S(1)}, u32[]{:S(2)}, u32[]{:S(2)}) async-start(f32[8,16,128]{2,1,0:T(8,128)} %fusion.38), calls=%async_computation.1 | async-start | bytes 131072 | tf_op jit(solution)/shard_map/all_to_all | solution.py:263
  68.3 5.2 %collective-permute-start.13 = (f32[8,128]{1,0:T(8,128)S(1)}, f32[8,128]{1,0:T(8,128)S(1)}, u32[]{:S(2)}, u32[]{:S(2)}) collective-permute-start(f32[8,128]{1,0:T(8,128)S(1)} %get-tuple-element.6), channel_id=1, source_target_pairs={{0,16},{16,0},{4,20},{20,4},{8,24},{24,8},{12,28},{28,12},{1,17},{... | collective-permute-start | bytes 12296 | tf_op jit(solution)/shard_map/ppermute | solution.py:37
  78.2 4.0 %collective-permute-start.15 = (f32[1,128]{1,0:T(1,128)S(1)}, f32[1,128]{1,0:T(1,128)S(1)}, u32[]{:S(2)}, u32[]{:S(2)}) collective-permute-start(f32[1,128]{1,0:T(1,128)S(1)} %get-tuple-element.189), channel_id=1, source_target_pairs={{1,0},{2,1},{3,2},{4,3},{5,4},{6,5},{7,6},{8,7},{9,8},{10,9},{11,1... | collective-permute-start | bytes 1544 | tf_op jit(solution)/shard_map/ppermute | solution.py:23
  80.9 6.6 %collective-permute-start.14 = (f32[1,128]{1,0:T(1,128)S(1)}, f32[1,128]{1,0:T(1,128)S(1)}, u32[]{:S(2)}, u32[]{:S(2)}) collective-permute-start(f32[1,128]{1,0:T(1,128)S(1)} %get-tuple-element.188), channel_id=1, source_target_pairs={{0,1},{1,2},{2,3},{3,4},{4,5},{5,6},{6,7},{7,8},{8,9},{9,10},{10,1... | collective-permute-start | bytes 1544 | tf_op jit(solution)/shard_map/ppermute | solution.py:21
  87.7 4.6 %collective-permute-start.16 = (f32[8,128]{1,0:T(8,128)S(1)}, f32[8,128]{1,0:T(8,128)S(1)}, u32[]{:S(2)}, u32[]{:S(2)}) collective-permute-start(f32[8,128]{1,0:T(8,128)S(1)} %fusion.190), channel_id=1, source_target_pairs={{0,16},{16,0},{4,20},{20,4},{8,24},{24,8},{12,28},{28,12},{1,17},{... | collective-permute-start | bytes 12296 | tf_op jit(solution)/shard_map/ppermute | solution.py:37
  96.9 1.4 collective-permute-start.18
  96.9 6.6 %collective-permute-start.17 = (f32[1,128]{1,0:T(1,128)S(1)}, f32[1,128]{1,0:T(1,128)S(1)}, u32[]{:S(2)}, u32[]{:S(2)}) collective-permute-start(f32[1,128]{1,0:T(1,128)S(1)} %get-tuple-element.178), channel_id=1, source_target_pairs={{0,1},{1,2},{2,3},{3,4},{4,5},{5,6},{6,7},{7,8},{8,9},{9,10},{10,1... | collective-permute-start | bytes 1544 | tf_op jit(solution)/shard_map/ppermute | solution.py:21
  103.8 4.6 %collective-permute-start.19 = (f32[8,128]{1,0:T(8,128)S(1)}, f32[8,128]{1,0:T(8,128)S(1)}, u32[]{:S(2)}, u32[]{:S(2)}) collective-permute-start(f32[8,128]{1,0:T(8,128)S(1)} %fusion.171), channel_id=1, source_target_pairs={{0,16},{16,0},{4,20},{20,4},{8,24},{24,8},{12,28},{28,12},{1,17},{... | collective-permute-start | bytes 12296 | tf_op jit(solution)/shard_map/ppermute | solution.py:37
  113.0 1.4 collective-permute-start.21
  113.1 6.6 %collective-permute-start.20 = (f32[1,128]{1,0:T(1,128)S(1)}, f32[1,128]{1,0:T(1,128)S(1)}, u32[]{:S(2)}, u32[]{:S(2)}) collective-permute-start(f32[1,128]{1,0:T(1,128)S(1)} %get-tuple-element.168), channel_id=1, source_target_pairs={{0,1},{1,2},{2,3},{3,4},{4,5},{5,6},{6,7},{7,8},{8,9},{9,10},{10,1... | collective-permute-start | bytes 1544 | tf_op jit(solution)/shard_map/ppermute | solution.py:21
  120.0 4.6 %collective-permute-start.22 = (f32[8,128]{1,0:T(8,128)S(1)}, f32[8,128]{1,0:T(8,128)S(1)}, u32[]{:S(2)}, u32[]{:S(2)}) collective-permute-start(f32[8,128]{1,0:T(8,128)S(1)} %fusion.152), channel_id=1, source_target_pairs={{0,16},{16,0},{4,20},{20,4},{8,24},{24,8},{12,28},{28,12},{1,17},{... | collective-permute-start | bytes 12296 | tf_op jit(solution)/shard_map/ppermute | solution.py:37
  129.2 1.4 collective-permute-start.24
  129.2 6.6 %collective-permute-start.23 = (f32[1,128]{1,0:T(1,128)S(1)}, f32[1,128]{1,0:T(1,128)S(1)}, u32[]{:S(2)}, u32[]{:S(2)}) collective-permute-start(f32[1,128]{1,0:T(1,128)S(1)} %get-tuple-element.158), channel_id=1, source_target_pairs={{0,1},{1,2},{2,3},{3,4},{4,5},{5,6},{6,7},{7,8},{8,9},{9,10},{10,1... | collective-permute-start | bytes 1544 | tf_op jit(solution)/shard_map/ppermute | solution.py:21
  136.1 4.6 %collective-permute-start.25 = (f32[8,128]{1,0:T(8,128)S(1)}, f32[8,128]{1,0:T(8,128)S(1)}, u32[]{:S(2)}, u32[]{:S(2)}) collective-permute-start(f32[8,128]{1,0:T(8,128)S(1)} %fusion.133), channel_id=1, source_target_pairs={{0,16},{16,0},{4,20},{20,4},{8,24},{24,8},{12,28},{28,12},{1,17},{... | collective-permute-start | bytes 12296 | tf_op jit(solution)/shard_map/ppermute | solution.py:37
  145.3 1.4 collective-permute-start.27
  145.4 6.6 %collective-permute-start.26 = (f32[1,128]{1,0:T(1,128)S(1)}, f32[1,128]{1,0:T(1,128)S(1)}, u32[]{:S(2)}, u32[]{:S(2)}) collective-permute-start(f32[1,128]{1,0:T(1,128)S(1)} %get-tuple-element.148), channel_id=1, source_target_pairs={{0,1},{1,2},{2,3},{3,4},{4,5},{5,6},{6,7},{7,8},{8,9},{9,10},{10,1... | collective-permute-start | bytes 1544 | tf_op jit(solution)/shard_map/ppermute | solution.py:21
  152.2 4.6 %collective-permute-start.28 = (f32[8,128]{1,0:T(8,128)S(1)}, f32[8,128]{1,0:T(8,128)S(1)}, u32[]{:S(2)}, u32[]{:S(2)}) collective-permute-start(f32[8,128]{1,0:T(8,128)S(1)} %fusion.114), channel_id=1, source_target_pairs={{0,16},{16,0},{4,20},{20,4},{8,24},{24,8},{12,28},{28,12},{1,17},{... | collective-permute-start | bytes 12296 | tf_op jit(solution)/shard_map/ppermute | solution.py:37
  161.5 1.4 collective-permute-start.30
  161.5 6.6 %collective-permute-start.29 = (f32[1,128]{1,0:T(1,128)S(1)}, f32[1,128]{1,0:T(1,128)S(1)}, u32[]{:S(2)}, u32[]{:S(2)}) collective-permute-start(f32[1,128]{1,0:T(1,128)S(1)} %get-tuple-element.138), channel_id=1, source_target_pairs={{0,1},{1,2},{2,3},{3,4},{4,5},{5,6},{6,7},{7,8},{8,9},{9,10},{10,1... | collective-permute-start | bytes 1544 | tf_op jit(solution)/shard_map/ppermute | solution.py:21
  168.4 4.6 %collective-permute-start.31 = (f32[8,128]{1,0:T(8,128)S(1)}, f32[8,128]{1,0:T(8,128)S(1)}, u32[]{:S(2)}, u32[]{:S(2)}) collective-permute-start(f32[8,128]{1,0:T(8,128)S(1)} %fusion.95), channel_id=1, source_target_pairs={{0,16},{16,0},{4,20},{20,4},{8,24},{24,8},{12,28},{28,12},{1,17},{... | collective-permute-start | bytes 12296 | tf_op jit(solution)/shard_map/ppermute | solution.py:37
  177.6 1.4 collective-permute-start.33
  177.7 6.6 %collective-permute-start.32 = (f32[1,128]{1,0:T(1,128)S(1)}, f32[1,128]{1,0:T(1,128)S(1)}, u32[]{:S(2)}, u32[]{:S(2)}) collective-permute-start(f32[1,128]{1,0:T(1,128)S(1)} %get-tuple-element.128), channel_id=1, source_target_pairs={{0,1},{1,2},{2,3},{3,4},{4,5},{5,6},{6,7},{7,8},{8,9},{9,10},{10,1... | collective-permute-start | bytes 1544 | tf_op jit(solution)/shard_map/ppermute | solution.py:21
  184.5 4.6 %collective-permute-start.34 = (f32[8,128]{1,0:T(8,128)S(1)}, f32[8,128]{1,0:T(8,128)S(1)}, u32[]{:S(2)}, u32[]{:S(2)}) collective-permute-start(f32[8,128]{1,0:T(8,128)S(1)} %fusion.76), channel_id=1, source_target_pairs={{0,16},{16,0},{4,20},{20,4},{8,24},{24,8},{12,28},{28,12},{1,17},{... | collective-permute-start | bytes 12296 | tf_op jit(solution)/shard_map/ppermute | solution.py:37
where the time goes:
time: 195 us; the launch traced here: 194 us
  waiting for transfers between devices  91 us (47%)
  starting transfers between devices  44.4 us (23%)
  local copies, waits for them, and re-layouts  42.9 us (22%)
  other arithmetic  11.9 us (6%)
  matrix products  2.65 us (1%)
    ppermute x13, waiting for transfers between devices, with_halo(): lax.ppermute(tail, axis, [(i, (i + 1) % count) for i in range(ends)])  44.2 us
    gather x8, local copies, waits for them, and re-layouts, couple(): mirrored = jnp.take_along_axis(partner_phi, columns, axis=-1)  36.3 us
    ppermute x9, waiting for transfers between devices, swapped(): return lax.ppermute(block, axis, route)  31.5 us
    ppermute x13, starting transfers between devices, with_halo(): lax.ppermute(tail, axis, [(i, (i + 1) % count) for i in range(ends)])  18.8 us
    ppermute x13, starting transfers between devices, with_halo(): lax.ppermute(head, axis, [((i + 1) % count, i) for i in range(ends)])  14.6 us
    all_to_all x1, waiting for transfers between devices, body(): lax.all_to_all(outgoing, 'gx', split_axis=0, concat_axis=0, tiled=True)  6.83 us
    ppermute x13, waiting for transfers between devices, with_halo(): lax.ppermute(head, axis, [((i + 1) % count, i) for i in range(ends)])  6.16 us
    gather x1, local copies, waits for them, and re-layouts, couple(): mirrored_ped = jnp.take_along_axis(partner_ped, columns, axis=-1)  4.54 us
  transfers between devices with their start and end apart: 37, of which 28 were waited for; matrix products, arithmetic and copies ran while one was open for 9% of the time, Pallas kernels for 0%

commit v1 on v0

v1 whole, which is shorter than its diff:
```python
import functools

import jax
import jax.numpy as jnp
from jax import lax
from jax.experimental import pallas as pl
from jax.experimental.pallas import tpu as pltpu
from jax.sharding import PartitionSpec as P

SWEEPS = 8
GAMMA = 5.0 / 3.0
COURANT = 0.08
PAD = 8
F32 = jnp.float32
MESH = pl.DeviceIdType.MESH


def cell_terms(prim):
    rho, vel, mag, pres = prim[0], prim[1:4], prim[4:7], prim[7]
    field_sq = mag[0] * mag[0] + mag[1] * mag[1] + mag[2] * mag[2]
    vel_sq = vel[0] * vel[0] + vel[1] * vel[1] + vel[2] * vel[2]
    half_sq = 0.5 * field_sq
    energy = pres * (1.0 / (GAMMA - 1.0)) + 0.5 * rho * vel_sq + half_sq
    total_p = pres + half_sq
    v_dot_b = vel[0] * mag[0] + vel[1] * mag[1] + vel[2] * mag[2]
    inv = 1.0 / rho
    sound_sq = GAMMA * pres * inv
    both = sound_sq + field_sq * inv
    momentum = [rho * v for v in vel]
    state = [rho] + momentum + list(mag) + [energy]
    return state, total_p, v_dot_b, sound_sq * inv, both


def flux_of(prim, terms, d):
    state, total_p, v_dot_b, sound_over, both = terms
    vel, mag = prim[1:4], prim[4:7]
    vn, bn = vel[d], mag[d]
    flux = [state[1 + d]]
    for e in range(3):
        m = state[1 + e] * vn - mag[e] * bn
        flux.append(m + total_p if e == d else m)
    for e in range(3):
        flux.append(None if e == d else mag[e] * vn - bn * vel[e])
    flux.append((state[7] + total_p) * vn - bn * v_dot_b)
    spread = both * both - 4.0 * sound_over * bn * bn
    fast = jnp.sqrt(0.5 * (both + jnp.sqrt(jnp.maximum(spread, 0.0))))
    return flux, jnp.abs(vn) + fast


def face(f_lo, f_hi, u_lo, u_hi, largest):
    jump = largest * (u_hi - u_lo)
    return -0.5 * jump if f_lo is None else 0.5 * ((f_lo + f_hi) - jump)


def roll(values, shift, axis):
    return pltpu.roll(values, shift % values.shape[axis], axis)


def kernel(sizes, rho, vel, mag, pres, owner, line_row, ped, hall, shift,
           out, phi_out,
           win, fwin, part, part_in, cwin, swin, shwin,
           loc_sem, xs, xr, ys, yr, cs, cr, fs, fr, as_, ar, ss, sr):
    nx, ny = sizes
    cx, cy, nz = rho.shape
    ri = ped.shape[0]
    g, p = lax.axis_index("gx"), lax.axis_index("pb")
    n = nx * ny
    half = n // 2
    b = g * ny + p

    def dev(flat):
        return (flat // ny, flat % ny)

    ion = [
        ((b + 1) % n, 0),
        ((b + n - 1) % n, 2),
        ((b + half + 1) % n, 3),
        ((b + half) % n, 4),
        ((b + half + n - 1) % n, 5),
    ]

    barrier = pltpu.get_barrier_semaphore()

    def greet(k, carry):
        pl.semaphore_signal(barrier, inc=1, device_id=((g + k) % nx, p), device_id_type=MESH)
        return carry

    lax.fori_loop(1, nx, greet, 0)
    for flat, slot in ion:
        if slot != 4:
            pl.semaphore_signal(barrier, inc=1, device_id=dev(flat), device_id_type=MESH)

    rows = pl.ds(PAD, cy)
    mid = pl.ds(1, cx)
    prims = [(rho, 0, 1), (vel, 1, 3), (mag, 4, 3), (pres, 7, 1)]
    local = []
    for i, (ref, at, count) in enumerate(prims):
        dst = win.at[at] if count == 1 else win.at[pl.ds(at, count)]
        dst = dst.at[mid, rows] if count == 1 else dst.at[:, mid, rows]
        local.append(pltpu.make_async_copy(ref, dst, loc_sem.at[i]))
    cond_local = [
        pltpu.make_async_copy(ped, cwin.at[0, 1], loc_sem.at[4]),
        pltpu.make_async_copy(hall, cwin.at[1, 1], loc_sem.at[5]),
    ]
    for c in local + cond_local:
        c.start()

    row8 = lax.broadcasted_iota(jnp.int32, (ri, nz), 0)
    sh = jnp.zeros((ri, nz), jnp.int32)
    for i in range(ri):
        sh = jnp.where(row8 == i, shift[i], sh)
    shwin[1] = sh

    pl.semaphore_wait(barrier, nx - 1 + 4)

    def remote(src, dst, send, recv, where):
        return pltpu.make_async_remote_copy(
            src_ref=src, dst_ref=dst, send_sem=send, recv_sem=recv,
            device_id=where, device_id_type=MESH)

    x_up, x_dn = (jnp.minimum(g + 1, nx - 1), p), (jnp.maximum(g - 1, 0), p)
    y_up, y_dn = (g, jnp.minimum(p + 1, ny - 1)), (g, jnp.maximum(p - 1, 0))
    has_xu, has_xd, has_yu, has_yd = g < nx - 1, g > 0, p < ny - 1, p > 0

    def halo_copies(srcs, wref, sends, recvs, is_x):
        both = []
        for way in range(2):
            copies = []
            for i, (ref, at, count, lead) in enumerate(srcs):
                if is_x:
                    s_at = (cx - 1 if way == 0 else 0) + lead[0]
                    d_at = 0 if way == 0 else cx + 1
                    r = pl.ds(lead[1], cy)
                    if count == 1:
                        src, dst = ref.at[s_at, r], wref.at[at, d_at, rows]
                    else:
                        src = ref.at[pl.ds(lead[2], count), s_at, r]
                        dst = wref.at[pl.ds(at, count), d_at, rows]
                    where = x_up if way == 0 else x_dn
                else:
                    s_at = (cy - PAD if way == 0 else 0) + lead[1]
                    d_at = 0 if way == 0 else PAD + cy
                    xs_ = pl.ds(lead[0], cx)
                    if count == 1:
                        src = ref.at[xs_, pl.ds(s_at, PAD)]
                        dst = wref.at[at, mid, pl.ds(d_at, PAD)]
                    else:
                        src = ref.at[pl.ds(lead[2], count), xs_, pl.ds(s_at, PAD)]
                        dst = wref.at[pl.ds(at, count), mid, pl.ds(d_at, PAD)]
                    where = y_up if way == 0 else y_dn
                copies.append(remote(src, dst, sends.at[way, i], recvs.at[way, i], where))
            both.append(copies)
        return both

    def each(cond, copies, act):
        @pl.when(cond)
        def _():
            for c in copies:
                getattr(c, act)()

    srcs = [(ref, at, count, (0, 0, 0)) for ref, at, count in prims]
    xc = halo_copies(srcs, win, xs, xr, True)
    yc = halo_copies(srcs, win, ys, yr, False)
    each(has_xu, xc[0], "start")
    each(has_xd, xc[1], "start")
    each(has_yu, yc[0], "start")
    each(has_yd, yc[1], "start")
    cond_copies = []
    for flat, slot in ion:
        cond_copies.append(remote(ped, cwin.at[0, slot], cs.at[0, slot], cr.at[0, slot], dev(flat)))
        cond_copies.append(remote(hall, cwin.at[1, slot], cs.at[1, slot], cr.at[1, slot], dev(flat)))
        if slot < 3:
            cond_copies.append(
                remote(shwin.at[1], shwin.at[slot], cs.at[2, slot], cr.at[2, slot], dev(flat)))
    for c in cond_copies:
        c.start()

    for c in local + cond_local:
        c.wait()

    lane = lax.broadcasted_iota(jnp.int32, (cx, cy, nz), 2)
    prim = [win[v, 1:1 + cx, PAD:PAD + cy, :] for v in range(8)]
    terms = cell_terms(prim)
    flux, speed = flux_of(prim, terms, 2)
    first, last = lane == 0, lane == nz - 1

    def z_dn(a):
        return jnp.where(first, a, roll(a, 1, 2))

    largest = jnp.maximum(speed, z_dn(speed))
    for v in range(8):
        u, f = terms[0][v], flux[v]
        low = face(None if f is None else z_dn(f), f, z_dn(u), u, largest)
        top = jnp.zeros_like(u) if f is None else f
        high = jnp.where(last, top, roll(low, -1, 2))
        out[v] = u - COURANT * (high - low)

    each(has_yd, yc[0], "wait_recv")
    each(has_yu, yc[1], "wait_recv")

    @pl.when(p == 0)
    def _():
        for v in range(8):
            win[v, 1:1 + cx, PAD - 1:PAD, :] = win[v, 1:1 + cx, PAD:PAD + 1, :]

    @pl.when(p == ny - 1)
    def _():
        for v in range(8):
            win[v, 1:1 + cx, PAD + cy:PAD + cy + 1, :] = win[v, 1:1 + cx, PAD + cy - 1:PAD + cy, :]

    prim = [win[v, 1:1 + cx] for v in range(8)]
    terms = cell_terms(prim)
    flux, speed = flux_of(prim, terms, 1)
    largest = jnp.maximum(speed, roll(speed, 1, 1))
    for v in range(8):
        u, f = terms[0][v], flux[v]
        low = face(None if f is None else roll(f, 1, 1), f, roll(u, 1, 1), u, largest)
        diff = roll(low, -1, 1) - low
        out[v] = out[v] - COURANT * diff[:, PAD:PAD + cy, :]

    each(has_xd, xc[0], "wait_recv")
    each(has_xu, xc[1], "wait_recv")

    @pl.when(g == 0)
    def _():
        for v in range(8):
            win[v, 0, PAD:PAD + cy, :] = win[v, 1, PAD:PAD + cy, :]

    @pl.when(g == nx - 1)
    def _():
        for v in range(8):
            win[v, cx + 1, PAD:PAD + cy, :] = win[v, cx, PAD:PAD + cy, :]

    prim = [win[v, :, PAD:PAD + cy, :] for v in range(8)]
    terms = cell_terms(prim)
    flux, speed = flux_of(prim, terms, 0)
    largest = jnp.maximum(speed[:-1], speed[1:])
    for v in (4, 6, 5, 0, 1, 2, 3, 7):
        u, f = terms[0][v], flux[v]
        lows = face(None if f is None else f[:-1], None if f is None else f[1:], u[:-1], u[1:], largest)
        new = out[v] - COURANT * (lows[1:] - lows[:-1])
        out[v] = new
        if 4 <= v <= 6:
            fwin[{4: 0, 6: 1, 5: 2}[v], 1:1 + cx, PAD:PAD + cy, :] = new
        if v == 5:
            fx = halo_copies([(fwin, 1, 2, (1, PAD, 1))], fwin, fs.at[0], fr.at[0], True)
            fy = halo_copies([(fwin, 0, 2, (1, PAD, 0))], fwin, fs.at[1], fr.at[1], False)
            each(has_xu, fx[0], "start")
            each(has_xd, fx[1], "start")
            each(has_yu, fy[0], "start")
            each(has_yd, fy[1], "start")

    each(has_xd, fx[0], "wait_recv")
    each(has_xu, fx[1], "wait_recv")
    each(has_yd, fy[0], "wait_recv")
    each(has_yu, fy[1], "wait_recv")

    @pl.when(g == 0)
    def _():
        for v in (1, 2):
            fwin[v, 0, PAD:PAD + cy, :] = fwin[v, 1, PAD:PAD + cy, :]

    @pl.when(g == nx - 1)
    def _():
        for v in (1, 2):
            fwin[v, cx + 1, PAD:PAD + cy, :] = fwin[v, cx, PAD:PAD + cy, :]

    @pl.when(p == 0)
    def _():
        for v in (0, 1):
            fwin[v, 1:1 + cx, PAD - 1:PAD, :] = fwin[v, 1:1 + cx, PAD:PAD + 1, :]

    @pl.when(p == ny - 1)
    def _():
        for v in (0, 1):
            fwin[v, 1:1 + cx, PAD + cy:PAD + cy + 1, :] = (
                fwin[v, 1:1 + cx, PAD + cy - 1:PAD + cy, :])

    def d_x(v):
        return 0.5 * (fwin[v, 2:2 + cx, PAD:PAD + cy, :] - fwin[v, 0:cx, PAD:PAD + cy, :])

    def d_y(v):
        a = fwin[v, 1:1 + cx]
        return 0.5 * (roll(a, -1, 1) - roll(a, 1, 1))[:, PAD:PAD + cy, :]

    def d_z(a):
        return 0.5 * (jnp.where(last, a, roll(a, -1, 2)) - z_dn(a))

    bx, bz, by = [fwin[v, 1:1 + cx, PAD:PAD + cy, :] for v in range(3)]
    jx = d_y(1) - d_z(by)
    jy = d_z(bx) - d_x(1)
    jz = d_x(2) - d_y(0)
    size = jnp.sqrt(bx * bx + by * by + bz * bz)
    current = (jx * bx + jy * by + jz * bz) / jnp.maximum(size, 1.0)
    current = current.reshape(cx * cy, nz)

    owners = owner[0, 0]
    row_hot = (lax.broadcasted_iota(jnp.int32, (ri, cx * cy), 0) == line_row[0]).astype(F32)

    def send_part(o, at):
        return remote(part.at[o], part_in.at[at], as_.at[o], ar.at[at], (o, p))

    def deposit(k, carry):
        o = (g + k) % nx
        mine = jnp.where(owners == o, current, 0.0)
        part[o] = jnp.dot(row_hot, mine, precision=lax.Precision.HIGHEST,
                          preferred_element_type=F32)

        @pl.when(k < nx)
        def _():
            send_part(o, g).start()

        return carry

    lax.fori_loop(1, nx + 1, deposit, 0, unroll=nx <= 8)

    for c in cond_copies:
        c.wait_recv()
    wide = 6 * ri
    row = lax.broadcasted_iota(jnp.int32, (wide, nz), 0)
    row = jnp.where(row >= 3 * ri, row - 3 * ri, row)
    place = b % half
    low_row = jnp.where(place == half // 2, ri, 0)
    high_row = jnp.where(place == half // 2 - 1, 2 * ri, 3 * ri)
    valid = (row >= low_row) & (row < high_row)
    pw = jnp.where(valid, cwin[0].reshape(wide, nz), 0.0)
    hw = jnp.where(valid, cwin[1].reshape(wide, nz), 0.0)
    own_shift = shwin[...].reshape(3 * ri, nz)
    col = lax.broadcasted_iota(jnp.int32, (3 * ri, nz), 1)
    cols = jnp.concatenate(
        [(col + own_shift) % nz, (col + (nz - own_shift)) % nz], axis=0)

    def swap(a):
        other = jnp.concatenate([a[3 * ri:], a[:3 * ri]], axis=0)
        return jnp.take_along_axis(other, cols, axis=1)

    def east(a):
        return roll(a, -1, 1)

    def west(a):
        return roll(a, 1, 1)

    def up(a):
        return roll(a, 1, 0)

    def down(a):
        return roll(a, -1, 0)

    he, hwst = east(hw), west(hw)
    coef = [
        0.5 * (pw + up(pw)), 0.5 * (pw + down(pw)),
        0.5 * (pw + east(pw)), 0.5 * (pw + west(pw)),
        0.125 * (hw + up(he)), 0.125 * (hw + up(hwst)),
        0.125 * (hw + down(he)), 0.125 * (hw + down(hwst)),
    ]
    center = coef[0]
    for c in coef[1:]:
        center = center + c
    inv = jnp.where(valid, 1.0 / jnp.where(valid, center, 1.0), 0.0)
    cu, cd, ce, cw, cue, cuw, cde, cdw = [c * inv for c in coef]
    pm = swap(pw)
    both = jnp.where(valid, pw + pm, 1.0)
    wa = jnp.where(valid, pw / both, 0.0)
    wb = jnp.where(valid, pm / both, 0.0)

    def take_part(k, total):
        s = (g + k) % nx
        send_part(s, s).wait_recv()
        return total + part_in[s]

    total = lax.fori_loop(1, nx, take_part, part[g], unroll=nx <= 8)
    swin[1] = total
    s_copies = [
        remote(swin.at[1], swin.at[slot], ss.at[slot], sr.at[slot], dev(flat)) for flat, slot in ion]
    for c in s_copies:
        c.start()
    for c in s_copies:
        c.wait_recv()
    source = swin[...].reshape(wide, nz) * inv

    def couple(phi):
        return wa * phi + wb * swap(phi)

    phi = couple(source)
    for _ in range(SWEEPS - 1):
        e, w = east(phi), west(phi)
        acc = source + ce * e + cw * w
        acc = acc + up_terms(phi, e, w, cu, cue, cuw, up)
        acc = acc + up_terms(phi, e, w, cd, -cde, -cdw, down)
        phi = couple(acc)
    phi_out[...] = phi[ri:2 * ri]

    each(has_xu, xc[0] + fx[0], "wait_send")
    each(has_xd, xc[1] + fx[1], "wait_send")
    each(has_yu, yc[0] + fy[0], "wait_send")
    each(has_yd, yc[1] + fy[1], "wait_send")
    for c in cond_copies + s_copies:
        c.wait_send()

    def sent(k, carry):
        send_part((g + k) % nx, g).wait_send()
        return carry

    lax.fori_loop(1, nx, sent, 0)


def up_terms(phi, e, w, straight, plus, minus, move):
    return straight * move(phi) + plus * move(e) - minus * move(w)


def body(sizes, density, velocity, magnetic, pressure, line_owner, line_row, pedersen, hall, mirror_shift):
    cx, cy, nz = density.shape
    ri = pedersen.shape[0]
    nx = sizes[0]
    any_ = pl.BlockSpec(memory_space=pl.ANY)
    vmem = pl.BlockSpec(memory_space=pltpu.VMEM)
    smem = pl.BlockSpec(memory_space=pltpu.SMEM)
    dma = pltpu.SemaphoreType.DMA
    return pl.pallas_call(
        functools.partial(kernel, sizes),
        out_shape=(
            jax.ShapeDtypeStruct((8, cx, cy, nz), F32),
            jax.ShapeDtypeStruct((ri, nz), F32),
        ),
        in_specs=[any_] * 4 + [vmem] * 2 + [any_] * 2 + [smem],
        out_specs=(vmem, vmem),
        scratch_shapes=[
            pltpu.VMEM((8, cx + 2, cy + 2 * PAD, nz), F32),
            pltpu.VMEM((3, cx + 2, cy + 2 * PAD, nz), F32),
            pltpu.VMEM((nx, ri, nz), F32),
            pltpu.VMEM((nx, ri, nz), F32),
            pltpu.VMEM((2, 6, ri, nz), F32),
            pltpu.VMEM((6, ri, nz), F32),
            pltpu.VMEM((3, ri, nz), jnp.int32),
            dma((6,)),
            dma((2, 4)), dma((2, 4)), dma((2, 4)), dma((2, 4)),
            dma((3, 6)), dma((3, 6)),
            dma((2, 2, 1)), dma((2, 2, 1)),
            dma((nx,)), dma((nx,)),
            dma((6,)), dma((6,)),
        ],
        compiler_params=pltpu.CompilerParams(collective_id=0, has_side_effects=True),
        name="flux_and_potential",
    )(density, velocity, magnetic, pressure, line_owner, line_row, pedersen, hall, mirror_shift)


def solution(mesh):
    sizes = (mesh.shape["gx"], mesh.shape["pb"])
    in_specs = (
        P("gx", "pb", None),
        P(None, "gx", "pb", None),
        P(None, "gx", "pb", None),
        P("gx", "pb", None),
        P("gx", "pb", None, None),
        P("gx", "pb", None),
        P(("gx", "pb"), None),
        P(("gx", "pb"), None),
        P(("gx", "pb")),
    )
    out_specs = (P(None, "gx", "pb", None), P(("gx", "pb"), None))
    return jax.shard_map(
        functools.partial(body, sizes), mesh=mesh, in_specs=in_specs, out_specs=out_specs,
        check_vma=False)
```

time: 195 us -> 32.9 us (0.17)
  waiting for transfers between devices: 91 us -> 0 us
  starting transfers between devices: 44.4 us -> 0 us
  local copies, waits for them, and re-layouts: 42.9 us -> 3.63 us
  Pallas kernels: 0 us -> 28.4 us
  other arithmetic: 11.9 us -> 0 us
  matrix products: 2.65 us -> 0 us
    ppermute x35 -> x0, waiting for transfers between devices: 81.8 us -> none  [the longest x13 44.2 us: with_halo(): lax.ppermute(tail, axis, [(i, (i + 1) % count) for i in range(ends)])]
    gather x9 -> x0, local copies, waits for them, and re-layouts: 40.8 us -> none  [the longest x8 36.3 us: couple(): mirrored = jnp.take_along_axis(partner_phi, columns, axis=-1)]
    ppermute x35 -> x0, starting transfers between devices: 37.3 us -> none  [the longest x13 18.8 us: with_halo(): lax.ppermute(tail, axis, [(i, (i + 1) % count) for i in range(ends)])]
    pallas_call x0 -> x1, Pallas kernels: none -> 28.4 us  [body(): pl.pallas_call(functools.partial(kernel, sizes), out_shape=(jax.ShapeDtyp...]
    all_to_all x2 -> x0, waiting for transfers between devices: 9.17 us -> none  [the longest x1 6.83 us: body(): lax.all_to_all(outgoing, 'gx', split_axis=0, concat_axis=0, tiled=True)]
    all_to_all x2 -> x0, starting transfers between devices: 7.05 us -> none  [the longest x1 3.62 us: body(): lax.all_to_all(outgoing, 'gx', split_axis=0, concat_axis=0, tiled=True)]
    concatenate x26 -> x0, other arithmetic: 3.83 us -> none  [the longest x2 1.05 us: pad_depth(): return jnp.pad(values, widths, mode='edge')]
    unnamed x16 -> x5, local copies, waits for them, and re-layouts: 0.05 us -> 3.63 us
  transfers between devices with their start and end apart: 37 -> 0, of which waited for: 28 -> 0; matrix products, arithmetic and copies ran while one was open for 9% -> 0% of each run, Pallas kernels for 0% -> 0%
where the time goes in v1:
time: 32.9 us; the launch traced here: 32.7 us
  Pallas kernels  28.4 us (86%)
  local copies, waits for them, and re-layouts  3.63 us (11%)
  between operations  0.65 us (2%)
    pallas_call x1, Pallas kernels, body(): pl.pallas_call(functools.partial(kernel, sizes), out_shape=(jax.ShapeDtyp...  28.4 us
    unnamed x5, local copies, waits for them, and re-layouts  3.63 us

profile of v1, /device:TPU:0, one launch (start us, length us, event | category | flops | bytes accessed | tf_op | source)
XLA Modules:
  0.0 32.7 jit_solution(15661153189083445040)
XLA Ops:
  0.6 1.4 %copy.11.owner = s32[1,1,64,1]{3,2,1,0:T(8,128)} copy(s32[1,1,64,1]{2,3,1,0:T(1,128)} %param.13) | data formatting | bytes 512 | tf_op args[4]
  2.0 28.4 %flux_and_potential.1 = (f32[8,2,32,128]{3,2,1,0:T(8,128)}, f32[8,128]{1,0:T(8,128)}) custom-call(f32[2,32,128]{2,1,0:T(8,128)} %rho.1, f32[3,2,32,128]{3,2,1,0:T(8,128)} %vel.1, f32[3,2,32,128]{3,2,1,0:T(8,128)} %mag.1, f32[2,32,128]{2,1,0:T(8,128)} %pres.1, s32[1,1,64,1]{3,2,1,0:T(8,128)} %copy.11.owner, s32[1,1,64]{2,1,0:T(1,128)} %line_row.1, ...), custom_call_target="tpu_custom_call" | custom-call | tf_op jit(solution)/shard_map/flux_and_potential/pallas_call | solution.py:419
  30.4 0.0 copy-start
  30.4 1.7 %copy.14 = f32[8,2,32,128]{3,2,1,0:T(8,128)} copy(f32[8,2,32,128]{3,2,1,0:T(8,128)} %get-tuple-element.4) | data formatting | bytes 524288
  32.1 0.0 copy-done
  32.1 0.6 %copy.15 = f32[8,128]{1,0:T(8,128)} copy(f32[8,128]{1,0:T(8,128)S(1)} %copy-done) | data formatting | bytes 8192
Async XLA Ops:
  30.4 1.7 %copy-start = (f32[8,128]{1,0:T(8,128)S(1)}, f32[8,128]{1,0:T(8,128)}, u32[]{:S(2)}) copy-start(f32[8,128]{1,0:T(8,128)} %get-tuple-element.5) | copy-start | bytes 12292

commit v2 on v1

--- a/solution.py
+++ b/solution.py
@@ -294,25 +294,26 @@
     current = (jx * bx + jy * by + jz * bz) / jnp.maximum(size, 1.0)
     current = current.reshape(cx * cy, nz)
 
-    owners = owner[0, 0]
-    row_hot = (lax.broadcasted_iota(jnp.int32, (ri, cx * cy), 0) == line_row[0]).astype(F32)
+    pairs = nx // 2
+    key = owner[0] * ri + line_row[0]
+    pair_row = lax.broadcasted_iota(jnp.int32, (2 * ri, cx * cy), 0)
+    pair_row = jnp.where(pair_row >= ri, pair_row + (pairs - 1) * ri, pair_row)
+
+    def deposit(q, carry):
+        hot = (key == pair_row + q * ri).astype(F32)
+        part[q] = jnp.dot(hot, current, precision=lax.Precision.HIGHEST,
+                          preferred_element_type=F32).reshape(2, ri, nz)
+        return carry
 
     def send_part(o, at):
-        return remote(part.at[o], part_in.at[at], as_.at[o], ar.at[at], (o, p))
-
-    def deposit(k, carry):
-        o = (g + k) % nx
-        mine = jnp.where(owners == o, current, 0.0)
-        part[o] = jnp.dot(row_hot, mine, precision=lax.Precision.HIGHEST,
-                          preferred_element_type=F32)
-
-        @pl.when(k < nx)
-        def _():
-            send_part(o, g).start()
-
+        return remote(part.at[o % pairs], part_in.at[at], as_.at[o], ar.at[at], (o, p))
+
+    def send(k, carry):
+        send_part((g + k) % nx, g).start()
         return carry
 
-    lax.fori_loop(1, nx + 1, deposit, 0, unroll=nx <= 8)
+    lax.fori_loop(0, pairs, deposit, 0, unroll=nx <= 8)
+    lax.fori_loop(1, nx, send, 0, unroll=nx <= 8)
 
     for c in cond_copies:
         c.wait_recv()
@@ -368,10 +369,13 @@
         send_part(s, s).wait_recv()
         return total + part_in[s]
 
-    total = lax.fori_loop(1, nx, take_part, part[g], unroll=nx <= 8)
-    swin[1] = total
+    total = lax.fori_loop(1, nx, take_part, part[g % pairs], unroll=nx <= 8)
+    northern = g < pairs
+    swin[0, 1] = jnp.where(northern, total[0], total[1])
+    swin[1, 1] = jnp.where(northern, total[1], total[0])
     s_copies = [
-        remote(swin.at[1], swin.at[slot], ss.at[slot], sr.at[slot], dev(flat)) for flat, slot in ion]
+        remote(swin.at[:, 1], swin.at[:, slot], ss.at[slot // 2], sr.at[slot // 2], dev(flat))
+        for flat, slot in ion[:2]]
     for c in s_copies:
         c.start()
     for c in s_copies:
@@ -419,29 +423,29 @@
     return pl.pallas_call(
         functools.partial(kernel, sizes),
         out_shape=(
-            jax.ShapeDtypeStruct((8, cx, cy, nz), F32),
-            jax.ShapeDtypeStruct((ri, nz), F32),
+            pltpu.VMEM((8, cx, cy, nz), F32),
+            pltpu.VMEM((ri, nz), F32),
         ),
         in_specs=[any_] * 4 + [vmem] * 2 + [any_] * 2 + [smem],
         out_specs=(vmem, vmem),
         scratch_shapes=[
             pltpu.VMEM((8, cx + 2, cy + 2 * PAD, nz), F32),
             pltpu.VMEM((3, cx + 2, cy + 2 * PAD, nz), F32),
-            pltpu.VMEM((nx, ri, nz), F32),
-            pltpu.VMEM((nx, ri, nz), F32),
+            pltpu.VMEM((nx // 2, 2, ri, nz), F32),
+            pltpu.VMEM((nx, 2, ri, nz), F32),
             pltpu.VMEM((2, 6, ri, nz), F32),
-            pltpu.VMEM((6, ri, nz), F32),
+            pltpu.VMEM((2, 3, ri, nz), F32),
             pltpu.VMEM((3, ri, nz), jnp.int32),
             dma((6,)),
             dma((2, 4)), dma((2, 4)), dma((2, 4)), dma((2, 4)),
             dma((3, 6)), dma((3, 6)),
             dma((2, 2, 1)), dma((2, 2, 1)),
             dma((nx,)), dma((nx,)),
-            dma((6,)), dma((6,)),
+            dma((2,)), dma((2,)),
         ],
         compiler_params=pltpu.CompilerParams(collective_id=0, has_side_effects=True),
         name="flux_and_potential",
-    )(density, velocity, magnetic, pressure, line_owner, line_row, pedersen, hall, mirror_shift)
+    )(density, velocity, magnetic, pressure, line_owner.reshape(1, 1, cx * cy), line_row, pedersen, hall, mirror_shift)
 
 
 def solution(mesh):

time: 32.9 us -> 28.8 us (0.88)
  local copies, waits for them, and re-layouts: 3.63 us -> 1.3 us
  Pallas kernels: 28.4 us -> 26.6 us
    unnamed x5 -> x2, local copies, waits for them, and re-layouts: 3.63 us -> 1.3 us
    pallas_call x1, Pallas kernels: 28.4 us -> 26.6 us  [body(): pl.pallas_call(functools.partial(kernel, sizes), out_shape=(pltpu.VMEM((8...]
where the time goes in v2:
time: 28.8 us; the launch traced here: 28.6 us
  Pallas kernels  26.6 us (92%)
  local copies, waits for them, and re-layouts  1.3 us (5%)
  between operations  0.64 us (2%)
    pallas_call x1, Pallas kernels, body(): pl.pallas_call(functools.partial(kernel, sizes), out_shape=(pltpu.VMEM((8...  26.6 us
    unnamed x2, local copies, waits for them, and re-layouts  1.3 us

profile of v2, /device:TPU:0, one launch (start us, length us, event | category | flops | bytes accessed | tf_op | source)
XLA Modules:
  0.0 28.6 jit_solution(4175960626570549893)
XLA Ops:
  0.6 26.6 %flux_and_potential.1 = (f32[8,2,32,128]{3,2,1,0:T(8,128)S(1)}, f32[8,128]{1,0:T(8,128)S(1)}) custom-call(f32[2,32,128]{2,1,0:T(8,128)} %rho.1, f32[3,2,32,128]{3,2,1,0:T(8,128)} %vel.1, f32[3,2,32,128]{3,2,1,0:T(8,128)} %mag.1, f32[2,32,128]{2,1,0:T(8,128)} %pres.1, s32[1,1,64]{2,1,0:T(1,128)} %bitcast.1, s32[1,1,64]{2,1,0:T(1,128)} %line_row.1, ...), custom_call_target="tpu_custom_call" | custom-call | tf_op jit(solution)/shard_map/flux_and_potential/pallas_call | solution.py:423
  27.3 0.7 %copy.13 = f32[8,2,32,128]{3,2,1,0:T(8,128)} copy(f32[8,2,32,128]{3,2,1,0:T(8,128)S(1)} %get-tuple-element.2) | data formatting | bytes 524288
  28.0 0.6 %copy.14 = f32[8,128]{1,0:T(8,128)} copy(f32[8,128]{1,0:T(8,128)S(1)} %get-tuple-element.3) | data formatting | bytes 8192

commit v3 on v2

--- a/solution.py
+++ b/solution.py
@@ -32,7 +32,7 @@
 
 
 def flux_of(prim, terms, d):
-    state, total_p, v_dot_b, sound_over, both = terms
+    state, total_p, v_dot_b = terms[:3]
     vel, mag = prim[1:4], prim[4:7]
     vn, bn = vel[d], mag[d]
     flux = [state[1 + d]]
@@ -42,9 +42,15 @@
     for e in range(3):
         flux.append(None if e == d else mag[e] * vn - bn * vel[e])
     flux.append((state[7] + total_p) * vn - bn * v_dot_b)
+    return flux
+
+
+def speed_of(prim, terms, d):
+    sound_over, both = terms[3:]
+    vn, bn = prim[1 + d], prim[4 + d]
     spread = both * both - 4.0 * sound_over * bn * bn
     fast = jnp.sqrt(0.5 * (both + jnp.sqrt(jnp.maximum(spread, 0.0))))
-    return flux, jnp.abs(vn) + fast
+    return jnp.abs(vn) + fast
 
 
 def face(f_lo, f_hi, u_lo, u_hi, largest):
@@ -122,11 +128,11 @@
     y_up, y_dn = (g, jnp.minimum(p + 1, ny - 1)), (g, jnp.maximum(p - 1, 0))
     has_xu, has_xd, has_yu, has_yd = g < nx - 1, g > 0, p < ny - 1, p > 0
 
-    def halo_copies(srcs, wref, sends, recvs, is_x):
+    def halo_copies(srcs, wref, sends, recvs, is_x, first_sem=0):
         both = []
         for way in range(2):
             copies = []
-            for i, (ref, at, count, lead) in enumerate(srcs):
+            for i, (ref, at, count, lead) in enumerate(srcs, first_sem):
                 if is_x:
                     s_at = (cx - 1 if way == 0 else 0) + lead[0]
                     d_at = 0 if way == 0 else cx + 1
@@ -159,7 +165,9 @@
                 getattr(c, act)()
 
     srcs = [(ref, at, count, (0, 0, 0)) for ref, at, count in prims]
-    xc = halo_copies(srcs, win, xs, xr, True)
+    xc = halo_copies(srcs[1:3], win, xs, xr, True)
+    xspeed = halo_copies([(win.at[8], 8, 1, (1, PAD, 0))], win, xs, xr, True, 2)
+    xlate = halo_copies([srcs[0], srcs[3]], win, xs, xr, True, 3)
     yc = halo_copies(srcs, win, ys, yr, False)
     each(has_xu, xc[0], "start")
     each(has_xd, xc[1], "start")
@@ -181,7 +189,10 @@
     lane = lax.broadcasted_iota(jnp.int32, (cx, cy, nz), 2)
     prim = [win[v, 1:1 + cx, PAD:PAD + cy, :] for v in range(8)]
     terms = cell_terms(prim)
-    flux, speed = flux_of(prim, terms, 2)
+    win[8, 1:1 + cx, PAD:PAD + cy, :] = speed_of(prim, terms, 0)
+    each(has_xu, xspeed[0], "start")
+    each(has_xd, xspeed[1], "start")
+    flux, speed = flux_of(prim, terms, 2), speed_of(prim, terms, 2)
     first, last = lane == 0, lane == nz - 1
 
     def z_dn(a):
@@ -210,7 +221,7 @@
 
     prim = [win[v, 1:1 + cx] for v in range(8)]
     terms = cell_terms(prim)
-    flux, speed = flux_of(prim, terms, 1)
+    flux, speed = flux_of(prim, terms, 1), speed_of(prim, terms, 1)
     largest = jnp.maximum(speed, roll(speed, 1, 1))
     for v in range(8):
         u, f = terms[0][v], flux[v]
@@ -218,30 +229,35 @@
         diff = roll(low, -1, 1) - low
         out[v] = out[v] - COURANT * diff[:, PAD:PAD + cy, :]
 
-    each(has_xd, xc[0], "wait_recv")
-    each(has_xu, xc[1], "wait_recv")
-
-    @pl.when(g == 0)
-    def _():
-        for v in range(8):
-            win[v, 0, PAD:PAD + cy, :] = win[v, 1, PAD:PAD + cy, :]
-
-    @pl.when(g == nx - 1)
-    def _():
-        for v in range(8):
-            win[v, cx + 1, PAD:PAD + cy, :] = win[v, cx, PAD:PAD + cy, :]
-
-    prim = [win[v, :, PAD:PAD + cy, :] for v in range(8)]
-    terms = cell_terms(prim)
-    flux, speed = flux_of(prim, terms, 0)
-    largest = jnp.maximum(speed[:-1], speed[1:])
-    for v in (4, 6, 5, 0, 1, 2, 3, 7):
-        u, f = terms[0][v], flux[v]
+    def edge_planes(which):
+        @pl.when(g == 0)
+        def _():
+            for v in which:
+                win[v, 0, PAD:PAD + cy, :] = win[v, 1, PAD:PAD + cy, :]
+
+        @pl.when(g == nx - 1)
+        def _():
+            for v in which:
+                win[v, cx + 1, PAD:PAD + cy, :] = win[v, cx, PAD:PAD + cy, :]
+
+    def planes(v):
+        return win[v, :, PAD:PAD + cy, :]
+
+    def x_change(u, f):
+        speed = planes(8)
+        largest = jnp.maximum(speed[:-1], speed[1:])
         lows = face(None if f is None else f[:-1], None if f is None else f[1:], u[:-1], u[1:], largest)
-        new = out[v] - COURANT * (lows[1:] - lows[:-1])
+        return COURANT * (lows[1:] - lows[:-1])
+
+    each(has_xd, xc[0] + xspeed[0], "wait_recv")
+    each(has_xu, xc[1] + xspeed[1], "wait_recv")
+    edge_planes((1, 2, 3, 4, 5, 6, 8))
+    for v in (4, 6, 5):
+        u = planes(v)
+        f = None if v == 4 else u * planes(1) - planes(4) * planes(v - 3)
+        new = out[v] - x_change(u, f)
         out[v] = new
-        if 4 <= v <= 6:
-            fwin[{4: 0, 6: 1, 5: 2}[v], 1:1 + cx, PAD:PAD + cy, :] = new
+        fwin[{4: 0, 6: 1, 5: 2}[v], 1:1 + cx, PAD:PAD + cy, :] = new
         if v == 5:
             fx = halo_copies([(fwin, 1, 2, (1, PAD, 1))], fwin, fs.at[0], fr.at[0], True)
             fy = halo_copies([(fwin, 0, 2, (1, PAD, 0))], fwin, fs.at[1], fr.at[1], False)
@@ -249,6 +265,8 @@
             each(has_xd, fx[1], "start")
             each(has_yu, fy[0], "start")
             each(has_yd, fy[1], "start")
+            each(has_xu, xlate[0], "start")
+            each(has_xd, xlate[1], "start")
 
     each(has_xd, fx[0], "wait_recv")
     each(has_xu, fx[1], "wait_recv")
@@ -364,6 +382,15 @@
     wa = jnp.where(valid, pw / both, 0.0)
     wb = jnp.where(valid, pm / both, 0.0)
 
+    each(has_xd, xlate[0], "wait_recv")
+    each(has_xu, xlate[1], "wait_recv")
+    edge_planes((0, 7))
+    prim = [planes(v) for v in range(8)]
+    terms = cell_terms(prim)
+    flux = flux_of(prim, terms, 0)
+    for v in (0, 1, 2, 3, 7):
+        out[v] = out[v] - x_change(terms[0][v], flux[v])
+
     def take_part(k, total):
         s = (g + k) % nx
         send_part(s, s).wait_recv()
@@ -394,8 +421,8 @@
         phi = couple(acc)
     phi_out[...] = phi[ri:2 * ri]
 
-    each(has_xu, xc[0] + fx[0], "wait_send")
-    each(has_xd, xc[1] + fx[1], "wait_send")
+    each(has_xu, xc[0] + xspeed[0] + xlate[0] + fx[0], "wait_send")
+    each(has_xd, xc[1] + xspeed[1] + xlate[1] + fx[1], "wait_send")
     each(has_yu, yc[0] + fy[0], "wait_send")
     each(has_yd, yc[1] + fy[1], "wait_send")
     for c in cond_copies + s_copies:
@@ -429,7 +456,7 @@
         in_specs=[any_] * 4 + [vmem] * 2 + [any_] * 2 + [smem],
         out_specs=(vmem, vmem),
         scratch_shapes=[
-            pltpu.VMEM((8, cx + 2, cy + 2 * PAD, nz), F32),
+            pltpu.VMEM((9, cx + 2, cy + 2 * PAD, nz), F32),
             pltpu.VMEM((3, cx + 2, cy + 2 * PAD, nz), F32),
             pltpu.VMEM((nx // 2, 2, ri, nz), F32),
             pltpu.VMEM((nx, 2, ri, nz), F32),
@@ -437,7 +464,7 @@
             pltpu.VMEM((2, 3, ri, nz), F32),
             pltpu.VMEM((3, ri, nz), jnp.int32),
             dma((6,)),
-            dma((2, 4)), dma((2, 4)), dma((2, 4)), dma((2, 4)),
+            dma((2, 5)), dma((2, 5)), dma((2, 4)), dma((2, 4)),
             dma((3, 6)), dma((3, 6)),
             dma((2, 2, 1)), dma((2, 2, 1)),
             dma((nx,)), dma((nx,)),

time: 28.8 us -> 28.3 us (0.983)
  Pallas kernels: 26.6 us -> 26.2 us
    pallas_call x1, Pallas kernels: 26.6 us -> 26.2 us  [body(): pl.pallas_call(functools.partial(kernel, sizes), out_shape=(pltpu.VMEM((8...]
where the time goes in v3:
time: 28.3 us; the launch traced here: 28.2 us
  Pallas kernels  26.2 us (93%)
  local copies, waits for them, and re-layouts  1.3 us (5%)
  between operations  0.64 us (2%)
    pallas_call x1, Pallas kernels, body(): pl.pallas_call(functools.partial(kernel, sizes), out_shape=(pltpu.VMEM((8...  26.2 us
    unnamed x2, local copies, waits for them, and re-layouts  1.3 us

profile of v3, /device:TPU:0, one launch (start us, length us, event | category | flops | bytes accessed | tf_op | source)
XLA Modules:
  0.0 28.2 jit_solution(13979137577329083395)
XLA Ops:
  0.6 26.2 %flux_and_potential.1 = (f32[8,2,32,128]{3,2,1,0:T(8,128)S(1)}, f32[8,128]{1,0:T(8,128)S(1)}) custom-call(f32[2,32,128]{2,1,0:T(8,128)} %rho.1, f32[3,2,32,128]{3,2,1,0:T(8,128)} %vel.1, f32[3,2,32,128]{3,2,1,0:T(8,128)} %mag.1, f32[2,32,128]{2,1,0:T(8,128)} %pres.1, s32[1,1,64]{2,1,0:T(1,128)} %bitcast.1, s32[1,1,64]{2,1,0:T(1,128)} %line_row.1, ...), custom_call_target="tpu_custom_call" | custom-call | tf_op jit(solution)/shard_map/flux_and_potential/pallas_call | solution.py:450
  26.9 0.7 %copy.13 = f32[8,2,32,128]{3,2,1,0:T(8,128)} copy(f32[8,2,32,128]{3,2,1,0:T(8,128)S(1)} %get-tuple-element.2) | data formatting | bytes 524288
  27.6 0.6 %copy.14 = f32[8,128]{1,0:T(8,128)} copy(f32[8,128]{1,0:T(8,128)S(1)} %get-tuple-element.3) | data formatting | bytes 8192
